TPU v7x, 128 devices: a whole 4x4x4 slice. The times are simulated.
128 devices in a mesh: row: 8 (over y, core), col: 16 (over z, x).
Axes of the slice: x: 4, y: 4, z: 4, core: 2. Of those that a mesh axis runs over, the one named last changes fastest.
Arguments:
- amplitudes: float32 [96, 256, 1024], P('col', None, 'row'), may hold values from -6 to 6
- interaction: float32 [16384, 16384], P('row', 'col'), may hold values from -0.5 to 0.5, as said below
- tile_counts: int32 [16], replicated, may hold values from 2 to 6, as said below
- tile_block: int32 [96], replicated, may hold values from -1 to 63, as said below
- recouple_sign: int32 [96], replicated, may hold values from 0 to 1
- orbit_perm: int32 [96, 256], replicated, may hold values from 0 to 255, each once within a row
- particle_energy: float32 [96, 256], P('col'), may hold values from -2 to 2
Outputs:
- sigma: float32 [96, 256, 1024], P('col', None, 'row')
Inputs may be any that keep to these rules, and one draw needn't show every extreme that they name: Owner c holds its live tiles in its first tile_counts[c] slots; the counts sum to 64, and some owner holds 6. `tile_block`: live slots map one to one onto the 64 cross-channel tiles, and slots that are not live hold -1; two live tiles of one owner never lie in the same aligned group of 4 cross-channel tiles. interaction equals its transpose.
All inputs are finite; a program needn't handle non-finite values.
Results may differ from a plain program's by a relative error of at most 0.000061.
Values sent between devices are 32-bit elements; how exact they have to be, the bound alone decides.
A program may use at most 128 MiB of HBM per device.

v0:
```python
import jax
import jax.numpy as jnp
from jax import lax
from jax.sharding import PartitionSpec as P


def split_up(value, dim, length):
    before, after = (value.shape[:dim], value.shape[dim + 1 :])
    return jnp.moveaxis(value.reshape(*before, length, -1, *after), dim, 0)


def sum_at_owner(value, axis, dim):
    length = lax.axis_size(axis)
    tiles = lax.all_to_all(split_up(value, dim, length), axis, 0, 0, tiled=True)
    return jnp.sum(tiles, axis=0)


def tile_recouple(tiles, phases, orders):
    moved = jax.vmap(lambda single, ordering: jnp.take(single, ordering, axis=0))(tiles, orders)
    return moved * phases[:, None, None]


def local(
    amplitudes, interaction, tile_counts, tile_block, recouple_sign, orbit_perm, particle_energy
):
    column_index = lax.axis_index("col")
    row_index = lax.axis_index("row")
    column_count = lax.axis_size("col")
    slots, tile_rows, narrow_cols = amplitudes.shape
    row_blocks = interaction.shape[0] // tile_rows
    col_blocks = interaction.shape[1] // tile_rows
    tile_total = tile_block.shape[0]
    slot_ids = jnp.arange(slots, dtype=jnp.int32)
    is_live = slot_ids < jnp.take(tile_counts, column_index)
    live_mask = is_live.astype(jnp.float32)[:, None, None]
    own_block = jnp.where(
        is_live, lax.dynamic_slice_in_dim(tile_block, column_index * slots, slots), -1
    )
    all_phases = (1 - 2 * recouple_sign).astype(jnp.float32)
    own_phases = lax.dynamic_slice_in_dim(all_phases, column_index * slots, slots)
    own_orders = lax.dynamic_slice_in_dim(orbit_perm, column_index * slots, slots, 0)
    diagonal = particle_energy[:, :, None] * amplitudes
    tile_ids = jnp.arange(tile_total, dtype=jnp.int32)
    peer_ids = jnp.arange(column_count, dtype=jnp.int32)

    def tiles_of(blocks):
        matches = tile_block[None, :] == blocks[:, None]
        return jnp.sum(jnp.where(matches, tile_ids[None, :], 0), axis=1)

    target_col = own_block // col_blocks
    my_blocks = column_index * col_blocks + jnp.arange(col_blocks, dtype=jnp.int32)
    block_tiles = tiles_of(my_blocks)
    widened = lax.all_gather(amplitudes, "row", axis=2, tiled=True)
    widened = tile_recouple(widened, own_phases, own_orders)
    group_blocks = row_index * row_blocks + jnp.arange(row_blocks, dtype=jnp.int32)
    group_tiles = tiles_of(group_blocks)
    is_owned = group_tiles // slots == column_index
    placed = (
        jnp.take(widened, group_tiles % slots, axis=0) * is_owned.astype(jnp.float32)[:, None, None]
    )
    crossed = lax.psum(placed.reshape(row_blocks * tile_rows, widened.shape[2]), "col")
    partial_cols = lax.dot_general(
        interaction,
        crossed,
        (((0,), (0,)), ((), ())),
        precision=lax.Precision.HIGHEST,
        preferred_element_type=jnp.float32,
    )
    own_part = sum_at_owner(partial_cols, "row", 1)
    blocks_here = own_part.reshape(col_blocks, tile_rows, narrow_cols)
    block_inverse = jnp.argsort(jnp.take(orbit_perm, block_tiles, axis=0), axis=1)
    blocks_here = tile_recouple(blocks_here, jnp.take(all_phases, block_tiles), block_inverse)
    block_owner = block_tiles // slots
    choose_mask = block_owner[None, :] == peer_ids[:, None]
    choose_block = jnp.sum(
        jnp.where(choose_mask, jnp.arange(col_blocks, dtype=jnp.int32)[None, :], 0), axis=1
    )
    choose_weight = jnp.max(choose_mask.astype(jnp.float32), axis=1)
    outgoing = jnp.take(blocks_here, choose_block, axis=0) * choose_weight[:, None, None]
    arrived = lax.all_to_all(outgoing, "col", split_axis=0, concat_axis=0, tiled=True)
    returned = jnp.take(arrived, jnp.clip(target_col, 0, column_count - 1), axis=0)
    return (returned + diagonal) * live_mask


def solution(mesh):
    placed = (P("col", None, "row"), P("row", "col"), P(), P(), P(), P(), P("col", None))
    return jax.shard_map(
        local, mesh=mesh, in_specs=placed, out_specs=P("col", None, "row"), check_vma=False
    )
```

profile of v0, /device:TPU:0, one launch (start us, length us, event | category | flops | bytes accessed | tf_op | source)
XLA Modules:
  0.0 392.9 jit_solution(7255663869322990882)
XLA Ops:
  7.4 0.0 all-gather.2.cloned.1.call-start
  7.4 0.7 all-gather.2.cloned.1.call-update
  8.1 0.0 all-reduce.2.cloned.1.call-start
  8.1 0.7 subtract_convert_fusion
  8.8 0.1 dynamic_slice.11
  8.9 0.7 bitcast_or_fusion
  9.6 0.8 select_reduce_fusion
  10.5 0.1 broadcast_bitcast_fusion
  10.6 0.1 broadcast_in_dim.144
  10.7 0.7 compare_and_fusion
  11.4 45.4 %all-gather.2.cloned.1.call-done = f32[6,256,1024]{2,1,0:T(8,128)} async-done(((f32[6,256,128]{2,1,0:T(8,128)}), f32[6,256,1024]{2,1,0:T(8,128)}) %all-gather.2.cloned.1.call-update) | async-done | bytes 6291472 | tf_op jit(solution)/shard_map/all_gather | solution.py:53
  56.8 30.4 %gather_fusion.5 = f32[1536,1024]{1,0:T(8,128)} fusion(f32[6,256,1024]{2,1,0:T(8,128)} %all-gather.2.cloned.1.call-done, s32[1536]{0:T(1024)S(1)} %reshape.221), kind=kCustom, calls=%fused_computation.5 | custom fusion | bytes 12595200 | tf_op jit(solution)/shard_map/vmap(jit(_take))/gather | solution.py:19
  87.2 4.9 %select_multiply_fusion = f32[6,256,1024]{2,1,0:T(8,128)} fusion(f32[6,256,1024]{2,1,0:T(8,128)} %bitcast.45, f32[6]{0:T(128)S(1)} %dynamic_slice.11, pred[6,256]{1,0:T(8,128)(4,1)S(1)} %compare_and_fusion), kind=kLoop, calls=%fused_computation.9 | loop fusion | flops 3145728 | bytes 12584472 | tf_op jit(solution)/shard_map/mul | solution.py:20
  92.1 7.1 %gather_fusion.1 = f32[8,256,1024]{2,1,0:T(8,128)} fusion(f32[6,256,1024]{2,1,0:T(8,128)} %select_multiply_fusion, s32[1024]{0:T(1024)S(1)} %pad_clamp_fusion.2), kind=kCustom, calls=%fused_computation.1 | custom fusion | bytes 16777248 | tf_op jit(solution)/shard_map/jit(_take)/gather | solution.py:59
  99.2 5.8 %fusion = f32[2048,1024]{1,0:T(8,128)} fusion(f32[8,256,1024]{2,1,0:T(8,128)} %gather_fusion.1, f32[2048]{0:T(1024)S(1)} %bitcast.48, pred[2048]{0:T(1024)(128)(4,1)S(1)} %broadcast_in_dim.145), kind=kLoop, calls=%fused_computation.8 | loop fusion | flops 4194304 | bytes 16787456 | tf_op jit(solution)/shard_map/mul | solution.py:59
  105.1 0.0 all-reduce.2.cloned.1.call-update
  105.1 142.9 %all-reduce.2.cloned.1.call-done = f32[2048,1024]{1,0:T(8,128)} async-done(((f32[2048,1024]{1,0:T(8,128)}), f32[2048,1024]{1,0:T(8,128)}) %all-reduce.2.cloned.1.call-update) | async-done | bytes 8388624 | tf_op jit(solution)/shard_map/psum | solution.py:61
  248.0 31.6 %fusion.5 = f32[1024,1024]{1,0:T(8,128)} fusion(f32[2048,1024]{1,0:T(8,128)} %all-reduce.2.cloned.1.call-done, f32[2048,1024]{1,0:T(8,128)} %param.8), kind=kOutput, calls=%fused_computation.61 | convolution fusion | flops 25769803776 | bytes 20971520 | tf_op jit(solution)/shard_map/dot_general | solution.py:62
  279.6 4.7 %all-to-all-start = ((f32[8,1024,128]{1,2,0:T(8,128)}), f32[8,1024,128]{1,2,0:T(8,128)}, u32[]{:S(2)}, u32[]{:S(2)}) async-start(f32[8,1024,128]{1,2,0:T(8,128)} %bitcast.46), calls=%async_computation | async-start | bytes 8388608 | tf_op jit(solution)/shard_map/all_to_all | solution.py:14
  284.3 0.2 sort.19.cloned.1.call-start
  284.6 0.2 select_reduce_fusion.2
  284.8 0.6 gather_fusion.2
  285.4 1.5 gather_fusion
  286.9 0.7 broadcast_select_fusion
  287.6 0.6 iota.37
  288.1 0.0 sort.19.cloned.1.call-update
  288.2 0.1 select_reduce_fusion.1
  288.3 0.1 convert_reduce_fusion
  288.4 2.7 sort.19.cloned.1.call-done
  291.1 0.7 fusion.1
  291.8 0.7 compare_and_fusion.1
  292.4 41.5 %all-to-all-done = f32[8,1024,128]{1,2,0:T(8,128)} async-done(((f32[8,1024,128]{1,2,0:T(8,128)}), f32[8,1024,128]{1,2,0:T(8,128)}, u32[]{:S(2)}, u32[]{:S(2)}) %all-to-all-start) | async-done | bytes 4194336 | tf_op jit(solution)/shard_map/all_to_all | solution.py:14
  334.0 2.6 reduce_sum.44
  336.6 0.2 copy.9
  336.8 6.8 %gather_fusion.6 = f32[1024,128]{1,0:T(8,128)S(1)} fusion(f32[4,256,128]{2,1,0:T(8,128)S(1)} %bitcast.44, s32[1024]{0:T(1024)S(1)} %bitcast.43), kind=kCustom, calls=%fused_computation.6 | custom fusion | bytes 1056768 | tf_op jit(solution)/shard_map/vmap(jit(_take))/gather | solution.py:19
  343.6 0.2 select_multiply_fusion.2
  343.8 0.0 copy-start.3
  343.8 0.0 copy-start
  343.8 0.0 copy-start.1
  343.8 0.7 gather_fusion.3
  344.5 1.6 select_multiply_fusion.1
  346.2 4.5 %all-to-all-start.1 = ((f32[16,256,128]{2,1,0:T(8,128)}), f32[16,256,128]{2,1,0:T(8,128)S(1)}, u32[]{:S(2)}, u32[]{:S(2)}) async-start(f32[16,256,128]{2,1,0:T(8,128)} %select_multiply_fusion.1), calls=%async_computation.1 | async-start | bytes 4194304 | tf_op jit(solution)/shard_map/all_to_all | solution.py:80
  350.7 0.6 dynamic-slice.2
  351.9 0.1 compare_and_fusion.5
  352.1 29.7 %all-to-all-done.1 = f32[16,256,128]{2,1,0:T(8,128)S(1)} async-done(((f32[16,256,128]{2,1,0:T(8,128)}), f32[16,256,128]{2,1,0:T(8,128)S(1)}, u32[]{:S(2)}, u32[]{:S(2)}) %all-to-all-start.1) | async-done | bytes 2097184 | tf_op jit(solution)/shard_map/all_to_all | solution.py:80
  381.7 1.5 gather_fusion.4
  383.2 0.0 copy-done
  383.2 2.3 add_multiply_fusion
  (21 shorter events, 0.1 us)
Async XLA Ops:
  7.4 49.4 %all-gather.2.cloned.1.call-start = ((), (), s32[]{:S(2)}) async-start(), calls=%async_computation.2 | async-start | bytes 7077888 | tf_op jit(solution)/shard_map/all_gather | solution.py:53
  8.1 239.9 %all-reduce.2.cloned.1.call-start = ((), (), s32[]{:S(2)}) async-start(), calls=%async_computation.3 | async-start | bytes 16777216 | tf_op jit(solution)/shard_map/psum | solution.py:61
  279.6 4.9 %copy-start.2 = (s32[96]{0:T(128)S(1)}, s32[96]{0:T(128)}, u32[]{:S(2)}) copy-start(s32[96]{0:T(128)} %param.10) | copy-start | bytes 1156
  279.6 54.3 %all-to-all-start = ((f32[8,1024,128]{1,2,0:T(8,128)}), f32[8,1024,128]{1,2,0:T(8,128)}, u32[]{:S(2)}, u32[]{:S(2)}) async-start(f32[8,1024,128]{1,2,0:T(8,128)} %bitcast.46), calls=%async_computation | async-start | bytes 8388608 | tf_op jit(solution)/shard_map/all_to_all | solution.py:14
  284.3 6.7 %sort.19.cloned.1.call-start = ((), (), s32[]{:S(2)}) async-start(), calls=%async_computation.4 | async-start | bytes 24608 | tf_op jit(solution)/shard_map/jit(argsort)/sort | solution.py:71
  343.8 6.9 %copy-start.3 = (s32[16]{0:T(128)S(1)}, s32[16]{0:T(128)}, u32[]{:S(2)}) copy-start(s32[16]{0:T(128)} %param.9) | copy-start | bytes 196
  343.8 39.4 %copy-start = (f32[6,256,128]{2,1,0:T(8,128)S(1)}, f32[6,256,128]{2,1,0:T(8,128)}, u32[]{:S(2)}) copy-start(f32[6,256,128]{2,1,0:T(8,128)} %param.7) | copy-start | bytes 2359300
  343.8 39.4 %copy-start.1 = (f32[6,256]{1,0:T(8,128)S(1)}, f32[6,256]{1,0:T(8,128)}, u32[]{:S(2)}) copy-start(f32[6,256]{1,0:T(8,128)} %param.13) | copy-start | bytes 18436
  346.2 35.5 %all-to-all-start.1 = ((f32[16,256,128]{2,1,0:T(8,128)}), f32[16,256,128]{2,1,0:T(8,128)S(1)}, u32[]{:S(2)}, u32[]{:S(2)}) async-start(f32[16,256,128]{2,1,0:T(8,128)} %select_multiply_fusion.1), calls=%async_computation.1 | async-start | bytes 4194304 | tf_op jit(solution)/shard_map/all_to_all | solution.py:80
Sparse Core Ops, SparseCore 0:
  9.8 46.9 all-gather.1
  105.2 142.7 all-reduce.1
Sparse Core Ops, SparseCore 1:
  288.3 2.5 sort.21.cloned.1.call-done
  (1 shorter events, 0.0 us)
where the time goes:
time: 394 us; the launch traced here: 393 us
  waiting for transfers between devices  260 us (66%)
  local copies, waits for them, and re-layouts  53.1 us (13%)
  matrix products  31.6 us (8%)
  other arithmetic  23.1 us (6%)
  between operations  15.6 us (4%)
  starting transfers between devices  9.24 us (2%)
    psum x1, waiting for transfers between devices, local(): lax.psum(placed.reshape(row_blocks * tile_rows, widened.shape[2]), 'col')  143 us
    all_gather x1, waiting for transfers between devices, local(): widened = lax.all_gather(amplitudes, 'row', axis=2, tiled=True)  45.4 us
    all_to_all x1, waiting for transfers between devices, sum_at_owner(): tiles = lax.all_to_all(split_up(value, dim, length), axis, 0, 0, tiled=True)  41.5 us
    gather x3, local copies, waits for them, and re-layouts, tile_recouple(): jnp.take(single, ordering, axis=0)  37.2 us
    dot_general x1, matrix products, local(): lax.dot_general(interaction, crossed, (((0,), (0,)), ((), ())), precision...  31.6 us
    all_to_all x1, waiting for transfers between devices, local(): lax.all_to_all(outgoing, 'col', split_axis=0, concat_axis=0, tiled=True)  29.7 us
  transfers between devices with their start and end apart: 4, of which 4 were waited for; matrix products, arithmetic and copies ran while one was open for 2% of the time, Pallas kernels for 0%

commit v1 on v0

v1 whole, which is shorter than its diff:
```python
import functools

import jax
import jax.numpy as jnp
from jax import lax
from jax.experimental import pallas as pl
from jax.experimental.pallas import tpu as pltpu
from jax.sharding import PartitionSpec as P

MESH = pl.DeviceIdType.MESH
F32, BF16 = jnp.float32, jnp.bfloat16
ROWS, COLS = 8, 16
SLOTS, TILE, LANES = 6, 256, 128
PIECE = TILE // COLS
STEPS = 4


def split3(v):
    a = v.astype(BF16)
    rest = v - a.astype(F32)
    b = rest.astype(BF16)
    d = (rest - b.astype(F32)).astype(BF16)
    return jnp.concatenate([a, b, d], axis=1)


def sum3(v):
    return v[:, :LANES] + v[:, LANES : 2 * LANES] + v[:, 2 * LANES :]


def kernel(
    counts, tblk, signs, tile_of, amp, perm, energy, w_hbm, out,
    onehot, send1, recv1, sel, xb, wst, whi, wlo, xhi, xlo, part, pin, rin,
    img, gb, ob, fin,
    wsem, s1, r1, s2, r2, sx, rx, sp, rp, sr, rr, s4, r4, s5, r5,
):
    row, col = lax.axis_index("row"), lax.axis_index("col")
    y, k = row // 2, row % 2
    z, x = col // 4, col % 4
    zp, zm, z2 = (z + 1) % 4, (z + 3) % 4, (z + 2) % 4
    xp, xm, x2 = (x + 1) % 4, (x + 3) % 4, (x + 2) % 4
    partner = row + 1 - 2 * k

    def rcopy(src, dst, ssem, rsem, to):
        return pltpu.make_async_remote_copy(
            src_ref=src, dst_ref=dst, send_sem=ssem, recv_sem=rsem,
            device_id=to, device_id_type=MESH,
        )

    barrier = pltpu.get_barrier_semaphore()

    @pl.loop(1, COLS)
    def _(d):
        pl.semaphore_signal(barrier, inc=1, device_id=(row, (col + d) % COLS), device_id_type=MESH)

    @pl.loop(1, ROWS)
    def _(d):
        pl.semaphore_signal(barrier, inc=1, device_id=((row + d) % ROWS, col), device_id_type=MESH)

    def wcopy(j):
        return pltpu.make_async_copy(w_hbm.at[:, j], wst.at[j], wsem.at[j])

    @pl.loop(0, COLS)
    def _(j):
        wcopy(j).start()

    row_iota = lax.broadcasted_iota(jnp.int32, (TILE, TILE), 0)
    col_iota = lax.broadcasted_iota(jnp.int32, (TILE, TILE), 1)

    @pl.loop(0, SLOTS)
    def _(s):
        order = perm[pl.ds(col * SLOTS + s, 1), :]
        phase = (1 - 2 * signs[col * SLOTS + s]).astype(F32)
        hot = jnp.where(row_iota == order, phase, 0.0)
        onehot[s] = hot.astype(BF16)
        moved = sum3(
            jnp.dot(hot.T.astype(BF16), split3(amp[s]), preferred_element_type=F32)
        )
        send1[:, pl.ds(s, 1)] = moved.reshape(COLS, 1, PIECE, LANES)

    pl.semaphore_wait(barrier, COLS - 1 + ROWS - 1)

    def spread_out(j):
        return rcopy(
            send1.at[j], recv1.at[pl.ds(col * SLOTS, SLOTS)], s1.at[j], r1.at[col], (row, j)
        )

    def spread_in(j):
        return rcopy(
            send1.at[j], recv1.at[pl.ds(j * SLOTS, SLOTS)], s1.at[j], r1.at[j], (row, j)
        )

    @pl.loop(1, COLS)
    def _(d):
        spread_out((col + d) % COLS).start()

    recv1[pl.ds(col * SLOTS, SLOTS)] = send1[col]

    @pl.loop(0, SLOTS)
    def _(s):
        diag = jnp.sum(
            jnp.where(row_iota == col_iota, energy[pl.ds(s, 1), :], 0.0), axis=1, keepdims=True
        )
        out[s] = diag * amp[s]

    @pl.loop(0, COLS // 2)
    def _(jp):
        wcopy(2 * jp).wait()
        wcopy(2 * jp + 1).wait()
        for mb in range(4):
            v = wst[pl.ds(2 * jp, 2), :, :, mb * TILE : (mb + 1) * TILE]
            v = v.reshape(TILE, TILE).T
            hi = v.astype(BF16)
            at = pl.ds(pl.multiple_of(jp * TILE, TILE), TILE)
            whi[mb * TILE : (mb + 1) * TILE, at] = hi
            wlo[mb * TILE : (mb + 1) * TILE, at] = (v - hi.astype(F32)).astype(BF16)

    @pl.loop(1, COLS)
    def _(d):
        spread_in((col + COLS - d) % COLS).wait_recv()

    @pl.loop(0, 64)
    def _(g):
        sel[g] = recv1[tile_of[g]]

    def rows_out(r):
        return rcopy(
            sel.at[pl.ds(r * 8, 8)], xb.at[row, z, x], s2.at[r], r2.at[row], (r, col)
        )

    def rows_in(r):
        return rcopy(sel.at[pl.ds(r * 8, 8)], xb.at[r, z, x], s2.at[r], r2.at[r], (r, col))

    @pl.loop(1, ROWS)
    def _(d):
        rows_out((row + d) % ROWS).start()

    xb[row, z, x] = sel[pl.ds(row * 8, 8)]

    @pl.loop(1, ROWS)
    def _(d):
        rows_in((row + d) % ROWS).wait_recv()

    def gather(s, kind, sends):
        h = 2 * ((y + 1 + s) % 4)
        g = h + 1
        refs = {
            (0, True): lambda: (xb.at[h, z, x], xb.at[h, z, x], xb.at[g, z, x], xb.at[g, z, x]),
            (0, False): lambda: (
                xb.at[h, z, xm], xb.at[h, z, xp], xb.at[g, zm, x], xb.at[g, zp, x]
            ),
            (1, True): lambda: (
                xb.at[h, z, xm, 0:4], xb.at[h, z, xp, 4:8],
                xb.at[g, zm, x, 0:4], xb.at[g, zp, x, 4:8],
            ),
            (1, False): lambda: (
                xb.at[h, z, x2, 0:4], xb.at[h, z, x2, 4:8],
                xb.at[g, z2, x, 0:4], xb.at[g, z2, x, 4:8],
            ),
            (2, True): lambda: (xb.at[h, z], xb.at[h, z], xb.at[g, :, x], xb.at[g, :, x]),
            (2, False): lambda: (xb.at[h, zm], xb.at[h, zp], xb.at[g, :, xm], xb.at[g, :, xp]),
            (3, True): lambda: (
                xb.at[h, zm, 0:2], xb.at[h, zp, 2:4], xb.at[g, 0:2, xm], xb.at[g, 2:4, xp]
            ),
            (3, False): lambda: (
                xb.at[h, z2, 0:2], xb.at[h, z2, 2:4], xb.at[g, 0:2, x2], xb.at[g, 2:4, x2]
            ),
        }[kind, sends]()
        along_x = ((row, z * 4 + xp), (row, z * 4 + xm))
        along_z = ((row, zp * 4 + x), (row, zm * 4 + x))
        to = along_x + along_z if kind < 2 else along_z + along_x
        return [
            rcopy(refs[n], refs[n], sx.at[s, kind, n], rx.at[s, kind, n], to[n])
            for n in range(4)
        ]

    def start(s, kind):
        for c in gather(s, kind, True):
            c.start()

    def arrived(s, kind):
        for c in gather(s, kind, False):
            c.wait_recv()

    @pl.loop(0, STEPS)
    def _(s):
        start(s, 0)

    @pl.loop(0, STEPS)
    def _(s):
        arrived(s, 0)
        start(s, 1)

    for s in range(2):
        arrived(s, 1)
        start(s, 2)
    arrived(0, 2)
    start(0, 3)

    def exchange(s):
        return rcopy(part.at[s, 1 - k], pin.at[s], sp.at[s], rp.at[s], (partner, col))

    def reduce_out(s):
        q = (y + 1 + s) % 4
        return rcopy(part.at[s, k], rin.at[s], sr.at[s], rr.at[s], (2 * q + k, col))

    def pair_sum(s):
        exchange(s).wait_recv()

        @pl.loop(0, 4)
        def _(m):
            at = pl.ds(m * TILE, TILE)
            part[s, k, at] = part[s, k, at] + pin[s, at]

        reduce_out(s).start()

    @pl.loop(0, STEPS)
    def _(s):
        @pl.when(s < STEPS - 2)
        def _():
            arrived(s + 2, 1)
            start(s + 2, 2)

        @pl.when(s < STEPS - 1)
        def _():
            arrived(s + 1, 2)
            start(s + 1, 3)

        @pl.when(s > 0)
        def _():
            pair_sum(s - 1)

        arrived(s, 3)
        h = 2 * ((y + 1 + s) % 4)

        @pl.loop(0, COLS // 2)
        def _(jp):
            at = (jp // 2, pl.ds(2 * (jp % 2), 2))
            va = xb[h, at[0], at[1]].reshape(TILE, LANES)
            vb = xb[h + 1, at[0], at[1]].reshape(TILE, LANES)
            v = jnp.concatenate([va, vb], axis=1)
            hi = v.astype(BF16)
            rows_at = pl.ds(pl.multiple_of(jp * TILE, TILE), TILE)
            xhi[rows_at, :] = hi
            xlo[rows_at, :] = (v - hi.astype(F32)).astype(BF16)

        @pl.loop(0, 4)
        def _(m):
            at = pl.ds(pl.multiple_of(m * TILE, TILE), TILE)
            acc = jnp.dot(whi[at, :], xlo[...], preferred_element_type=F32)
            acc += jnp.dot(wlo[at, :], xhi[...], preferred_element_type=F32)
            acc += jnp.dot(whi[at, :], xhi[...], preferred_element_type=F32)
            part[s, 0, at] = acc[:, :LANES]
            part[s, 1, at] = acc[:, LANES:]

        exchange(s).start()

    for s in range(STEPS - 1):
        reduce_out(s).wait_recv()
    exchange(STEPS - 1).wait_recv()

    @pl.loop(0, 4)
    def _(b):
        at = pl.ds(b * TILE, TILE)
        last = STEPS - 1
        v = part[last, k, at] + pin[last, at] + rin[0, at] + rin[1, at] + rin[2, at]
        img[:, pl.ds(b, 1)] = v.reshape(COLS, 1, PIECE, LANES)

    def back_out(j):
        return rcopy(img.at[j], gb.at[pl.ds(col * 4, 4)], s4.at[j], r4.at[col], (row, j))

    def back_in(j):
        return rcopy(img.at[j], gb.at[pl.ds(j * 4, 4)], s4.at[j], r4.at[j], (row, j))

    @pl.loop(1, COLS)
    def _(d):
        back_out((col + d) % COLS).start()

    gb[pl.ds(col * 4, 4)] = img[col]

    @pl.loop(1, COLS)
    def _(d):
        back_in((col + COLS - d) % COLS).wait_recv()

    @pl.loop(0, COLS * SLOTS)
    def _(i):
        ob[i] = gb[tblk[i]]

    def home_out(j):
        return rcopy(
            ob.at[pl.ds(j * SLOTS, SLOTS)], fin.at[col], s5.at[j], r5.at[col], (row, j)
        )

    def home_in(j):
        return rcopy(ob.at[pl.ds(j * SLOTS, SLOTS)], fin.at[j], s5.at[j], r5.at[j], (row, j))

    @pl.loop(1, COLS)
    def _(d):
        home_out((col + d) % COLS).start()

    fin[col] = ob[pl.ds(col * SLOTS, SLOTS)]

    @pl.loop(1, COLS)
    def _(d):
        home_in((col + COLS - d) % COLS).wait_recv()

    @pl.loop(0, SLOTS)
    def _(s):
        live = (s < counts[col]).astype(F32)
        v = fin[:, pl.ds(s, 1)].reshape(TILE, LANES)
        returned = sum3(jnp.dot(onehot[s], split3(v), preferred_element_type=F32))
        out[s] = (returned + out[s]) * live

    @pl.loop(1, COLS)
    def _(d):
        j = (col + d) % COLS
        spread_out(j).wait_send()
        back_out(j).wait_send()
        home_out(j).wait_send()

    @pl.loop(1, ROWS)
    def _(d):
        rows_out((row + d) % ROWS).wait_send()

    @pl.loop(0, STEPS)
    def _(s):
        for kind in range(4):
            for c in gather(s, kind, True):
                c.wait_send()
        exchange(s).wait_send()

    @pl.loop(0, STEPS - 1)
    def _(s):
        reduce_out(s).wait_send()


def local(
    amplitudes, interaction, tile_counts, tile_block, recouple_sign, orbit_perm, particle_energy
):
    tiles = jnp.arange(64, dtype=jnp.int32)
    slots = jnp.arange(COLS * SLOTS, dtype=jnp.int32)
    hit = tile_block[None, :] == tiles[:, None]
    tile_of = jnp.sum(jnp.where(hit, slots[None, :], 0), axis=1)
    tblk = jnp.clip(tile_block, 0, 63)
    w = interaction.reshape(8, COLS, PIECE, 1024)
    smem = pl.BlockSpec(memory_space=pltpu.SMEM)
    vmem = pl.BlockSpec(memory_space=pltpu.VMEM)
    dma = pltpu.SemaphoreType.DMA
    return pl.pallas_call(
        kernel,
        out_shape=jax.ShapeDtypeStruct(amplitudes.shape, F32),
        in_specs=[smem] * 4 + [vmem] * 3 + [pl.BlockSpec(memory_space=pl.ANY)],
        out_specs=vmem,
        scratch_shapes=[
            pltpu.VMEM((SLOTS, TILE, TILE), BF16),
            pltpu.VMEM((COLS, SLOTS, PIECE, LANES), F32),
            pltpu.VMEM((COLS * SLOTS, PIECE, LANES), F32),
            pltpu.VMEM((64, PIECE, LANES), F32),
            pltpu.VMEM((ROWS, 4, 4, 8, PIECE, LANES), F32),
            pltpu.VMEM((COLS, 8, PIECE, 1024), F32),
            pltpu.VMEM((1024, 2048), BF16),
            pltpu.VMEM((1024, 2048), BF16),
            pltpu.VMEM((2048, TILE), BF16),
            pltpu.VMEM((2048, TILE), BF16),
            pltpu.VMEM((STEPS, 2, 1024, LANES), F32),
            pltpu.VMEM((STEPS, 1024, LANES), F32),
            pltpu.VMEM((STEPS - 1, 1024, LANES), F32),
            pltpu.VMEM((COLS, 4, PIECE, LANES), F32),
            pltpu.VMEM((64, PIECE, LANES), F32),
            pltpu.VMEM((COLS * SLOTS, PIECE, LANES), F32),
            pltpu.VMEM((COLS, SLOTS, PIECE, LANES), F32),
            dma((COLS,)),
            dma((COLS,)), dma((COLS,)),
            dma((ROWS,)), dma((ROWS,)),
            dma((STEPS, 4, 4)), dma((STEPS, 4, 4)),
            dma((STEPS,)), dma((STEPS,)),
            dma((STEPS - 1,)), dma((STEPS - 1,)),
            dma((COLS,)), dma((COLS,)),
            dma((COLS,)), dma((COLS,)),
        ],
        compiler_params=pltpu.CompilerParams(
            collective_id=0, has_side_effects=True, vmem_limit_bytes=60 * 1024 * 1024
        ),
        name="sigma_step",
    )(tile_counts, tblk, recouple_sign, tile_of, amplitudes, orbit_perm, particle_energy, w)


def solution(mesh):
    placed = (P("col", None, "row"), P("row", "col"), P(), P(), P(), P(), P("col", None))
    return jax.shard_map(
        local, mesh=mesh, in_specs=placed, out_specs=P("col", None, "row"), check_vma=False
    )
```

time: 394 us -> 123 us (0.31)
  waiting for transfers between devices: 260 us -> 0 us
  Pallas kernels: 0 us -> 117 us
  local copies, waits for them, and re-layouts: 53.1 us -> 2.06 us
  matrix products: 31.6 us -> 0 us
  other arithmetic: 23.1 us -> 2.51 us
  between operations: 15.6 us -> 0.01 us
  starting transfers between devices: 9.24 us -> 0 us
    psum x1 -> x0, waiting for transfers between devices: 143 us -> none  [local(): lax.psum(placed.reshape(row_blocks * tile_rows, widened.shape[2]), 'col')]
    pallas_call x0 -> x1, Pallas kernels: none -> 117 us  [local(): pl.pallas_call(kernel, out_shape=jax.ShapeDtypeStruct(amplitudes.shape, F...]
    all_to_all x2 -> x0, waiting for transfers between devices: 71.2 us -> none  [the longest x1 41.5 us: sum_at_owner(): tiles = lax.all_to_all(split_up(value, dim, length), axis, 0, 0, tiled=True)]
    gather x8 -> x0, local copies, waits for them, and re-layouts: 48.6 us -> none  [the longest x3 37.2 us: tile_recouple(): jnp.take(single, ordering, axis=0)]
    all_gather x1 -> x0, waiting for transfers between devices: 45.4 us -> none  [local(): widened = lax.all_gather(amplitudes, 'row', axis=2, tiled=True)]
    dot_general x1 -> x0, matrix products: 31.6 us -> none  [local(): lax.dot_general(interaction, crossed, (((0,), (0,)), ((), ())), precision...]
    mul x5 -> x0, other arithmetic: 14.9 us -> none  [the longest x1 5.84 us: local(): jnp.take(widened, group_tiles % slots, axis=0)]
    all_to_all x2 -> x0, starting transfers between devices: 9.2 us -> none  [the longest x1 4.68 us: sum_at_owner(): tiles = lax.all_to_all(split_up(value, dim, length), axis, 0, 0, tiled=True)]
  transfers between devices with their start and end apart: 4 -> 0, of which waited for: 4 -> 0; matrix products, arithmetic and copies ran while one was open for 2% -> 0% of each run, Pallas kernels for 0% -> 0%
where the time goes in v1:
time: 123 us; the launch traced here: 122 us
  Pallas kernels  117 us (95%)
  other arithmetic  2.51 us (2%)
  local copies, waits for them, and re-layouts  2.06 us (2%)
    pallas_call x1, Pallas kernels, local(): pl.pallas_call(kernel, out_shape=jax.ShapeDtypeStruct(amplitudes.shape, F...  117 us

profile of v1, /device:TPU:0, one launch (start us, length us, event | category | flops | bytes accessed | tf_op | source)
XLA Modules:
  0.0 122.0 jit_solution(11202725441604896390)
XLA Ops:
  0.0 1.3 %select_reduce_fusion.tile_of = s32[64]{0:T(128)} fusion(s32[96]{0:T(128)} %param.10), kind=kLoop, calls=%fused_computation | loop fusion | flops 18368 | bytes 640 | tf_op jit(solution)/shard_map/reduce_sum | solution.py:342
  1.3 1.2 broadcast_clamp_fusion.tblk
  2.5 117.4 %sigma_step.1 = f32[6,256,128]{2,1,0:T(8,128)} custom-call(s32[16]{0:T(128)} %counts.1, s32[96]{0:T(128)} %broadcast_clamp_fusion.tblk, s32[96]{0:T(128)} %signs.1, s32[64]{0:T(128)} %select_reduce_fusion.tile_of, f32[6,256,128]{2,1,0:T(8,128)} %amp.1, s32[96,256]{1,0:T(8,128)} %perm.1, f32[6,256]{1,0:T(8,128)} %energy.1, f32[8,16,16,1024]{3,2,1,0:T(8,128)} %bitcast.1), custom_call_target="tpu_custom_call" | custom-call | tf_op jit(solution)/shard_map/sigma_step/pallas_call | solution.py:348
  119.9 2.1 %copy.9 = f32[6,256,128]{2,1,0:T(8,128)} copy(f32[6,256,128]{2,1,0:T(8,128)} %sigma_step.1) | data formatting | bytes 1572864

commit v2 on v1

v2 whole, which is shorter than its diff:
```python
import functools

import jax
import jax.numpy as jnp
from jax import lax
from jax.experimental import pallas as pl
from jax.experimental.pallas import tpu as pltpu
from jax.sharding import PartitionSpec as P

MESH = pl.DeviceIdType.MESH
F32, BF16 = jnp.float32, jnp.bfloat16
ROWS, COLS = 8, 16
SLOTS, TILE, LANES = 6, 256, 128
PIECE = TILE // COLS
STEPS = 4
HALF = 512


def split3(v):
    a = v.astype(BF16)
    rest = v - a.astype(F32)
    b = rest.astype(BF16)
    d = (rest - b.astype(F32)).astype(BF16)
    return jnp.concatenate([a, b, d], axis=1)


def sum3(v):
    return v[:, :LANES] + v[:, LANES : 2 * LANES] + v[:, 2 * LANES :]


def kernel(
    counts, tblk, signs, tile_of, amp, perm, energy, w_hbm, out,
    onehot, send1, recv1, sel, xb, wst, whi, wlo, xhi, xlo, part, pin, relay, rin,
    img, gb0, gb1, ob, fin,
    wsem, s1, r1, s2, r2, sx, rx, sp, rp, sy, ry, sr, rr, s4, r4, s5, r5,
):
    row, col = lax.axis_index("row"), lax.axis_index("col")
    y, k = row // 2, row % 2
    z, x = col // 4, col % 4
    zp, zm, z2 = (z + 1) % 4, (z + 3) % 4, (z + 2) % 4
    xp, xm, x2 = (x + 1) % 4, (x + 3) % 4, (x + 2) % 4
    yp, ym, y2 = (y + 1) % 4, (y + 3) % 4, (y + 2) % 4
    partner = row + 1 - 2 * k
    last = STEPS - 1
    held = (gb0, gb1)

    def rcopy(src, dst, ssem, rsem, to):
        return pltpu.make_async_remote_copy(
            src_ref=src, dst_ref=dst, send_sem=ssem, recv_sem=rsem,
            device_id=to, device_id_type=MESH,
        )

    barrier = pltpu.get_barrier_semaphore()

    @pl.loop(1, COLS)
    def _(d):
        pl.semaphore_signal(barrier, inc=1, device_id=(row, (col + d) % COLS), device_id_type=MESH)

    @pl.loop(1, ROWS)
    def _(d):
        pl.semaphore_signal(barrier, inc=1, device_id=((row + d) % ROWS, col), device_id_type=MESH)

    def wcopy(j):
        return pltpu.make_async_copy(w_hbm.at[:, j], wst.at[j], wsem.at[j])

    @pl.loop(0, COLS)
    def _(j):
        wcopy(j).start()

    row_iota = lax.broadcasted_iota(jnp.int32, (TILE, TILE), 0)
    col_iota = lax.broadcasted_iota(jnp.int32, (TILE, TILE), 1)

    @pl.loop(0, SLOTS)
    def _(s):
        order = perm[pl.ds(col * SLOTS + s, 1), :]
        phase = (1 - 2 * signs[col * SLOTS + s]).astype(F32)
        hot = jnp.where(row_iota == order, phase, 0.0)
        onehot[s] = hot.astype(BF16)
        moved = sum3(
            jnp.dot(hot.T.astype(BF16), split3(amp[s]), preferred_element_type=F32)
        )
        send1[:, pl.ds(s, 1)] = moved.reshape(COLS, 1, PIECE, LANES)

    pl.semaphore_wait(barrier, COLS - 1 + ROWS - 1)

    def spread(j, slot):
        return rcopy(
            send1.at[j], recv1.at[pl.ds(slot * SLOTS, SLOTS)], s1.at[j], r1.at[slot], (row, j)
        )

    @pl.loop(1, COLS)
    def _(d):
        spread((col + d) % COLS, col).start()

    recv1[pl.ds(col * SLOTS, SLOTS)] = send1[col]

    @pl.loop(0, COLS // 2)
    def _(jp):
        wcopy(2 * jp).wait()
        wcopy(2 * jp + 1).wait()
        at = pl.ds(pl.multiple_of(jp * TILE, TILE), TILE)
        for b in range(4):
            v = wst[pl.ds(2 * jp, 2), :, :, b * TILE : (b + 1) * TILE]
            v = v.reshape(TILE, TILE).T
            hi = v.astype(BF16)
            lo = (v - hi.astype(F32)).astype(BF16)
            for m in range(2):
                rows_at = slice(m * HALF + b * LANES, m * HALF + (b + 1) * LANES)
                whi[rows_at, at] = hi[m * LANES : (m + 1) * LANES]
                wlo[rows_at, at] = lo[m * LANES : (m + 1) * LANES]

    @pl.loop(1, COLS)
    def _(d):
        j = (col + COLS - d) % COLS
        spread(j, j).wait_recv()

    @pl.loop(0, 64, unroll=8)
    def _(g):
        sel[g] = recv1[tile_of[g]]

    def rows_copy(r, slot):
        return rcopy(
            sel.at[pl.ds(r * 8, 8)], xb.at[slot, z, x], s2.at[r], r2.at[slot], (r, col)
        )

    for r in (2 * y2, 2 * y2 + 1, 2 * yp, 2 * ym, 2 * yp + 1, 2 * ym + 1, partner):
        rows_copy(r, row).start()

    xb[row, z, x] = sel[pl.ds(row * 8, 8)]

    def rows_arrived(*rs):
        for r in rs:
            rows_copy(r, r).wait_recv()

    chunk = (
        (2 * y2, 2 * y2 + 1), (2 * yp, 2 * ym), (2 * yp + 1, 2 * ym + 1), (2 * y, 2 * y + 1),
    )
    to_x = ((row, z * 4 + xp), (row, z * 4 + xm))
    to_z = ((row, zp * 4 + x), (row, zm * 4 + x))

    def gather(s, kind, sends):
        h, g = chunk[s]
        lo, up = slice(0, 2), slice(2, 4)
        refs = {
            (0, True): lambda: (xb.at[h, z, x], xb.at[h, z, x], xb.at[g, z, x], xb.at[g, z, x]),
            (0, False): lambda: (
                xb.at[h, z, xm], xb.at[h, z, xp], xb.at[g, zm, x], xb.at[g, zp, x]
            ),
            (1, True): lambda: (
                xb.at[h, z, xm, 0:4], xb.at[h, z, xp, 4:8],
                xb.at[g, zm, x, 0:4], xb.at[g, zp, x, 4:8],
            ),
            (1, False): lambda: (
                xb.at[h, z, x2, 0:4], xb.at[h, z, x2, 4:8],
                xb.at[g, z2, x, 0:4], xb.at[g, z2, x, 4:8],
            ),
            (2, True): lambda: (
                xb.at[h, z, lo], xb.at[h, z, up], xb.at[g, lo, x], xb.at[g, up, x]
            ),
            (2, False): lambda: (
                xb.at[h, zm, lo], xb.at[h, zp, up], xb.at[g, lo, xm], xb.at[g, up, xp]
            ),
            (3, True): lambda: (
                xb.at[h, z, up], xb.at[h, z, lo], xb.at[g, up, x], xb.at[g, lo, x]
            ),
            (3, False): lambda: (
                xb.at[h, zm, up], xb.at[h, zp, lo], xb.at[g, up, xm], xb.at[g, lo, xp]
            ),
            (4, True): lambda: (
                xb.at[h, zm, lo], xb.at[h, zp, up], xb.at[g, lo, xm], xb.at[g, up, xp]
            ),
            (4, False): lambda: (
                xb.at[h, z2, lo], xb.at[h, z2, up], xb.at[g, lo, x2], xb.at[g, up, x2]
            ),
        }[kind, sends]()
        to = to_x + to_z if kind < 2 else to_z + to_x
        return [
            rcopy(refs[n], refs[n], sx.at[s, kind, n], rx.at[s, kind, n], to[n])
            for n in range(4)
        ]

    def start(s, *kinds):
        for kind in kinds:
            for c in gather(s, kind, True):
                c.start()

    def arrived(s, *kinds):
        for kind in kinds:
            for c in gather(s, kind, False):
                c.wait_recv()

    def exchange(s, m):
        return rcopy(
            part.at[s, 1 - k, m], pin.at[s, m], sp.at[s, m], rp.at[s, m], (partner, col)
        )

    def relay_copy(m, slot, to):
        return rcopy(part.at[0, k, m], relay.at[slot], sy.at[m], ry.at[slot], to)

    def relay_out(m):
        return relay_copy(m, k, (2 * yp, col) if m == 0 else (2 * ym + 1, col))

    def relay_in(slot):
        return relay_copy(0, slot, (partner, col))

    def reduce_out(s, m):
        q = yp + k * (ym - yp)
        return rcopy(
            part.at[s, k, m], rin.at[k, m], sr.at[s - 1, m], rr.at[k, m], (2 * q + s - 1, col)
        )

    def reduce_in(n, m):
        return rcopy(part.at[1, k, m], rin.at[n, m], sr.at[0, m], rr.at[n, m], (partner, col))

    def dots(s, m):
        @pl.loop(0, 2)
        def _(n):
            at = pl.ds(pl.multiple_of(m * HALF + n * TILE, TILE), TILE)
            to = pl.ds(pl.multiple_of(n * TILE, TILE), TILE)
            acc = jnp.dot(whi[at, :], xlo[...], preferred_element_type=F32)
            acc += jnp.dot(wlo[at, :], xhi[...], preferred_element_type=F32)
            acc += jnp.dot(whi[at, :], xhi[...], preferred_element_type=F32)
            part[s, 0, m, to] = acc[:, :LANES]
            part[s, 1, m, to] = acc[:, LANES:]

        exchange(s, m).start()

    def convert(s):
        h, g = chunk[s]

        @pl.loop(0, COLS // 2)
        def _(jp):
            pair = pl.ds(2 * (jp % 2), 2)
            va = xb[h, jp // 2, pair].reshape(TILE, LANES)
            vb = xb[g, jp // 2, pair].reshape(TILE, LANES)
            v = jnp.concatenate([va, vb], axis=1)
            hi = v.astype(BF16)
            at = pl.ds(pl.multiple_of(jp * TILE, TILE), TILE)
            xhi[at, :] = hi
            xlo[at, :] = (v - hi.astype(F32)).astype(BF16)

    def back(m, j, slot):
        return rcopy(
            img.at[m, j], held[m].at[pl.ds(slot * 4, 4)], s4.at[m, j], r4.at[m, slot], (row, j)
        )

    def home(m, j, slot):
        return rcopy(
            ob.at[m, pl.ds(j * SLOTS, SLOTS)], fin.at[m, slot], s5.at[m, j], r5.at[m, slot],
            (row, j),
        )

    def finish(m):
        exchange(last, m).wait_recv()
        reduce_in(0, m).wait_recv()
        reduce_in(1, m).wait_recv()
        v = part[last, k, m] + pin[last, m] + rin[0, m] + rin[1, m]
        v = v.reshape(4, COLS, 1, 8, LANES)
        for b in range(4):
            img[m, :, b : b + 1] = v[b]

        @pl.loop(1, COLS)
        def _(d):
            back(m, (col + d) % COLS, col).start()

        held[m][pl.ds(col * 4, 4)] = img[m, col]

    def send_home(m):
        @pl.loop(1, COLS)
        def _(d):
            j = (col + COLS - d) % COLS
            back(m, j, j).wait_recv()

        @pl.loop(0, COLS * SLOTS, unroll=8)
        def _(i):
            ob[m, i] = held[m][jnp.maximum(tblk[i], 0)]

        @pl.loop(1, COLS)
        def _(d):
            home(m, (col + d) % COLS, col).start()

        fin[m, col] = ob[m, pl.ds(col * SLOTS, SLOTS)]

    rows_arrived(partner)
    start(3, 0)
    rows_arrived(2 * y2, 2 * y2 + 1)
    start(0, 0)
    rows_arrived(2 * yp, 2 * ym)
    start(1, 0)
    arrived(3, 0)
    start(3, 1)
    arrived(0, 0)
    start(0, 1)
    rows_arrived(2 * yp + 1, 2 * ym + 1)
    start(2, 0)
    arrived(0, 1)
    start(0, 2, 3)
    arrived(1, 0)
    start(1, 1)
    arrived(2, 0)
    start(2, 1)
    arrived(1, 1)
    start(1, 2, 3)
    arrived(0, 2)
    start(0, 4)

    for s in range(STEPS):
        if s + 2 < STEPS:
            arrived(s + 2, 1)
            start(s + 2, 2, 3)
        if s + 1 < STEPS:
            arrived(s + 1, 2)
            start(s + 1, 4)
        arrived(s, 3, 4)
        convert(s)
        if s == last:
            for m in range(2):
                dots(s, m)
                finish(m)
            break
        dots(s, 0)
        dots(s, 1)
        for m in range(2):
            exchange(s, m).wait_recv()
            part[s, k, m] = part[s, k, m] + pin[s, m]
            if s == 0:
                relay_out(m).start()
        if s > 0:
            relay_in(s - 1).wait_recv()
            part[s, k, k] = part[s, k, k] + relay[s - 1]
            for m in range(2):
                reduce_out(s, m).start()

    send_home(0)
    send_home(1)

    @pl.loop(0, SLOTS)
    def _(s):
        diag = jnp.sum(
            jnp.where(row_iota == col_iota, energy[pl.ds(s, 1), :], 0.0), axis=1, keepdims=True
        )
        out[s] = diag * amp[s]

    for m in range(2):
        @pl.loop(1, COLS)
        def _(d):
            j = (col + COLS - d) % COLS
            home(m, j, j).wait_recv()

    @pl.loop(0, SLOTS)
    def _(s):
        live = (s < counts[col]).astype(F32)
        v = fin[:, :, pl.ds(s, 1)].reshape(TILE, LANES)
        returned = sum3(jnp.dot(onehot[s], split3(v), preferred_element_type=F32))
        out[s] = (returned + out[s]) * live

    @pl.loop(1, COLS)
    def _(d):
        j = (col + d) % COLS
        spread(j, col).wait_send()
        for m in range(2):
            back(m, j, col).wait_send()
            home(m, j, col).wait_send()

    @pl.loop(1, ROWS)
    def _(d):
        rows_copy((row + d) % ROWS, row).wait_send()

    for s in range(STEPS):
        for kind in range(5):
            for c in gather(s, kind, True):
                c.wait_send()
        for m in range(2):
            exchange(s, m).wait_send()
    for m in range(2):
        relay_out(m).wait_send()
        for s in (1, 2):
            reduce_out(s, m).wait_send()


def local(
    amplitudes, interaction, tile_counts, tile_block, recouple_sign, orbit_perm, particle_energy
):
    tiles = jnp.arange(64, dtype=jnp.int32)
    slots = jnp.arange(COLS * SLOTS, dtype=jnp.int32)
    hit = tile_block[None, :] == tiles[:, None]
    tile_of = jnp.sum(jnp.where(hit, slots[None, :], 0), axis=1)
    w = interaction.reshape(8, COLS, PIECE, 1024)
    smem = pl.BlockSpec(memory_space=pltpu.SMEM)
    vmem = pl.BlockSpec(memory_space=pltpu.VMEM)
    dma = pltpu.SemaphoreType.DMA
    return pl.pallas_call(
        kernel,
        out_shape=jax.ShapeDtypeStruct(amplitudes.shape, F32),
        in_specs=[smem] * 4 + [vmem] * 3 + [pl.BlockSpec(memory_space=pl.ANY)],
        out_specs=vmem,
        scratch_shapes=[
            pltpu.VMEM((SLOTS, TILE, TILE), BF16),
            pltpu.VMEM((COLS, SLOTS, PIECE, LANES), F32),
            pltpu.VMEM((COLS * SLOTS, PIECE, LANES), F32),
            pltpu.VMEM((64, PIECE, LANES), F32),
            pltpu.VMEM((ROWS, 4, 4, 8, PIECE, LANES), F32),
            pltpu.VMEM((COLS, 8, PIECE, 1024), F32),
            pltpu.VMEM((1024, 2048), BF16),
            pltpu.VMEM((1024, 2048), BF16),
            pltpu.VMEM((2048, TILE), BF16),
            pltpu.VMEM((2048, TILE), BF16),
            pltpu.VMEM((STEPS, 2, 2, HALF, LANES), F32),
            pltpu.VMEM((STEPS, 2, HALF, LANES), F32),
            pltpu.VMEM((2, HALF, LANES), F32),
            pltpu.VMEM((2, 2, HALF, LANES), F32),
            pltpu.VMEM((2, COLS, 4, 8, LANES), F32),
            pltpu.VMEM((64, 8, LANES), F32),
            pltpu.VMEM((64, 8, LANES), F32),
            pltpu.VMEM((2, COLS * SLOTS, 8, LANES), F32),
            pltpu.VMEM((2, COLS, SLOTS, 8, LANES), F32),
            dma((COLS,)),
            dma((COLS,)), dma((COLS,)),
            dma((ROWS,)), dma((ROWS,)),
            dma((STEPS, 5, 4)), dma((STEPS, 5, 4)),
            dma((STEPS, 2)), dma((STEPS, 2)),
            dma((2,)), dma((2,)),
            dma((2, 2)), dma((2, 2)),
            dma((2, COLS)), dma((2, COLS)),
            dma((2, COLS)), dma((2, COLS)),
        ],
        compiler_params=pltpu.CompilerParams(
            collective_id=0, has_side_effects=True, vmem_limit_bytes=60 * 1024 * 1024
        ),
        name="sigma_step",
    )(tile_counts, tile_block, recouple_sign, tile_of, amplitudes, orbit_perm, particle_energy, w)


def solution(mesh):
    placed = (P("col", None, "row"), P("row", "col"), P(), P(), P(), P(), P("col", None))
    return jax.shard_map(
        local, mesh=mesh, in_specs=placed, out_specs=P("col", None, "row"), check_vma=False
    )
```

time: 123 us -> 109 us (0.89)
  Pallas kernels: 117 us -> 105 us
    pallas_call x1, Pallas kernels: 117 us -> 105 us  [local(): pl.pallas_call(kernel, out_shape=jax.ShapeDtypeStruct(amplitudes.shape, F...]
where the time goes in v2:
time: 109 us
  Pallas kernels  105 us (96%)
  local copies, waits for them, and re-layouts  2.06 us (2%)
  other arithmetic  1.28 us (1%)
    pallas_call x1, Pallas kernels, local(): pl.pallas_call(kernel, out_shape=jax.ShapeDtypeStruct(amplitudes.shape, F...  105 us

profile of v2, /device:TPU:0, one launch (start us, length us, event | category | flops | bytes accessed | tf_op | source)
XLA Modules:
  0.0 108.6 jit_solution(9541311527455466614)
XLA Ops:
  0.0 1.3 %select_reduce_fusion.tile_of = s32[64]{0:T(128)} fusion(s32[96]{0:T(128)} %tblk.1), kind=kLoop, calls=%fused_computation | loop fusion | flops 18368 | bytes 640 | tf_op jit(solution)/shard_map/reduce_sum | solution.py:387
  1.3 105.2 %sigma_step.1 = f32[6,256,128]{2,1,0:T(8,128)} custom-call(s32[16]{0:T(128)} %counts.1, s32[96]{0:T(128)} %tblk.1, s32[96]{0:T(128)} %signs.1, s32[64]{0:T(128)} %select_reduce_fusion.tile_of, f32[6,256,128]{2,1,0:T(8,128)} %amp.1, s32[96,256]{1,0:T(8,128)} %perm.1, f32[6,256]{1,0:T(8,128)} %energy.1, f32[8,16,16,1024]{3,2,1,0:T(8,128)} %bitcast.1), custom_call_target="tpu_custom_call" | custom-call | tf_op jit(solution)/shard_map/sigma_step/pallas_call | solution.py:392
  106.5 2.1 %copy.9 = f32[6,256,128]{2,1,0:T(8,128)} copy(f32[6,256,128]{2,1,0:T(8,128)} %sigma_step.1) | data formatting | bytes 1572864

commit v3 on v2

v3 whole, which is shorter than its diff:
```python
import functools

import jax
import jax.numpy as jnp
from jax import lax
from jax.experimental import pallas as pl
from jax.experimental.pallas import tpu as pltpu
from jax.sharding import PartitionSpec as P

MESH = pl.DeviceIdType.MESH
F32, BF16 = jnp.float32, jnp.bfloat16
ROWS, COLS = 8, 16
SLOTS, TILE, LANES = 6, 256, 128
PIECE = TILE // COLS
STEPS = 4
HALF = 512


def split3(v):
    a = v.astype(BF16)
    rest = v - a.astype(F32)
    b = rest.astype(BF16)
    d = (rest - b.astype(F32)).astype(BF16)
    return jnp.concatenate([a, b, d], axis=1)


def sum3(v):
    return v[:, :LANES] + v[:, LANES : 2 * LANES] + v[:, 2 * LANES :]


def kernel(
    counts, tblk, signs, tile_of, amp, perm, energy, w_hbm, out,
    onehot, send1, recv1, sel, xa, xc, wst, whi, wlo, xhi, xlo, part, pin, relay, rin,
    img, gb0, gb1, ob, fin,
    wsem, s1, r1, s2, r2, sx, rx, sp, rp, sy, ry, sr, rr, s4, r4, s5, r5,
):
    row, col = lax.axis_index("row"), lax.axis_index("col")
    y, k = row // 2, row % 2
    z, x = col // 4, col % 4
    zp, zm, z2 = (z + 1) % 4, (z + 3) % 4, (z + 2) % 4
    xp, xm, x2 = (x + 1) % 4, (x + 3) % 4, (x + 2) % 4
    yp, ym, y2 = (y + 1) % 4, (y + 3) % 4, (y + 2) % 4
    partner = row + 1 - 2 * k
    last = STEPS - 1
    held = (gb0, gb1)

    def rcopy(src, dst, ssem, rsem, to):
        return pltpu.make_async_remote_copy(
            src_ref=src, dst_ref=dst, send_sem=ssem, recv_sem=rsem,
            device_id=to, device_id_type=MESH,
        )

    barrier = pltpu.get_barrier_semaphore()

    @pl.loop(1, COLS)
    def _(d):
        pl.semaphore_signal(barrier, inc=1, device_id=(row, (col + d) % COLS), device_id_type=MESH)

    @pl.loop(1, ROWS)
    def _(d):
        pl.semaphore_signal(barrier, inc=1, device_id=((row + d) % ROWS, col), device_id_type=MESH)

    def wcopy(j):
        return pltpu.make_async_copy(w_hbm.at[:, j], wst.at[j // 4, j % 4], wsem.at[j])

    @pl.loop(0, COLS)
    def _(j):
        wcopy(j).start()

    row_iota = lax.broadcasted_iota(jnp.int32, (TILE, TILE), 0)
    col_iota = lax.broadcasted_iota(jnp.int32, (TILE, TILE), 1)

    @pl.loop(0, SLOTS)
    def _(s):
        order = perm[pl.ds(col * SLOTS + s, 1), :]
        phase = (1 - 2 * signs[col * SLOTS + s]).astype(F32)
        hot = jnp.where(row_iota == order, phase, 0.0)
        onehot[s] = hot.astype(BF16)
        moved = sum3(
            jnp.dot(hot.T.astype(BF16), split3(amp[s]), preferred_element_type=F32)
        )
        send1[:, pl.ds(s, 1)] = moved.reshape(COLS, 1, PIECE, LANES)

    pl.semaphore_wait(barrier, COLS - 1 + ROWS - 1)

    def spread(j, slot):
        return rcopy(
            send1.at[j], recv1.at[pl.ds(slot * SLOTS, SLOTS)], s1.at[j], r1.at[slot], (row, j)
        )

    @pl.loop(1, COLS)
    def _(d):
        spread((col + d) % COLS, col).start()

    recv1[pl.ds(col * SLOTS, SLOTS)] = send1[col]

    @pl.loop(0, COLS)
    def _(j):
        wcopy(j).wait()

    def shift_of(n):
        return n + n // 2 - 2 * (n // 3)

    def place_a(n):
        return pl.ds(pl.multiple_of((n + 3 * (n // 3)) * TILE, TILE), TILE)

    def place_c(n):
        return pl.ds(pl.multiple_of((n + 3 + n // 3) * TILE, TILE), TILE)

    def weights(v, b, at):
        v = v.reshape(TILE, TILE).T
        hi = v.astype(BF16)
        lo = (v - hi.astype(F32)).astype(BF16)
        for m in range(2):
            rows_at = slice(m * HALF + b * LANES, m * HALF + (b + 1) * LANES)
            whi[rows_at, at] = hi[m * LANES : (m + 1) * LANES]
            wlo[rows_at, at] = lo[m * LANES : (m + 1) * LANES]

    @pl.loop(0, 4)
    def _(n):
        zn, xn = (z + shift_of(n)) % 4, (x + shift_of(n)) % 4
        for b in range(4):
            cut = slice(b * TILE, (b + 1) * TILE)
            weights(wst[zn, :, 0:4, :, cut], b, place_a(n))
            weights(wst[:, xn, 4:8, :, cut], b, place_c(n))

    @pl.loop(1, COLS)
    def _(d):
        j = (col + COLS - d) % COLS
        spread(j, j).wait_recv()

    @pl.loop(0, 64, unroll=8)
    def _(g):
        sel[g] = recv1[tile_of[g]]

    def rows_copies(r, source, slot):
        return [
            rcopy(
                sel.at[pl.ds(r * 8, 4)], xa.at[slot[0], z, x, slot[1]],
                s2.at[r, 0], r2.at[source, 0], (r, col),
            ),
            rcopy(
                sel.at[pl.ds(r * 8 + 4, 4)], xc.at[slot[0], x, z, slot[1]],
                s2.at[r, 1], r2.at[source, 1], (r, col),
            ),
        ]

    rows_sent = [
        c
        for r, slot in (
            (2 * y2, (0, k)), (2 * y2 + 1, (0, k)),
            (2 * ym, (1 + k, 0)), (2 * yp, (1 + k, 1)),
            (2 * ym + 1, (1 + k, 0)), (2 * yp + 1, (1 + k, 1)),
            (partner, (3, k)),
        )
        for c in rows_copies(r, row, slot)
    ]
    for c in rows_sent:
        c.start()

    xa[3, z, x, k] = sel[pl.ds(row * 8, 4)]
    xc[3, x, z, k] = sel[pl.ds(row * 8 + 4, 4)]

    def rows_arrived(s):
        for r, slot in (
            ((2 * y2, (0, 0)), (2 * y2 + 1, (0, 1))),
            ((2 * yp, (1, 0)), (2 * ym, (1, 1))),
            ((2 * yp + 1, (2, 0)), (2 * ym + 1, (2, 1))),
            ((partner, (3, 1 - k)),),
        )[s]:
            for c in rows_copies(r, r, slot):
                c.wait_recv()

    to_x = ((row, z * 4 + xp), (row, z * 4 + xm))
    to_z = ((row, zp * 4 + x), (row, zm * 4 + x))

    def gather(s, kind, sends):
        lo, up = slice(0, 2), slice(2, 4)
        if kind == 0:
            here, there = ((z, x), (z, x), (x, z), (x, z)), ((z, xm), (z, xp), (x, zm), (x, zp))
        elif kind == 1:
            here = ((z, xm, 0), (z, xp, 1), (x, zm, 0), (x, zp, 1))
            there = ((z, x2, 0), (z, x2, 1), (x, z2, 0), (x, z2, 1))
        elif kind == 2:
            here = ((z, lo), (z, up), (x, lo), (x, up))
            there = ((zm, lo), (zp, up), (xm, lo), (xp, up))
        elif kind == 3:
            here = ((z, up), (z, lo), (x, up), (x, lo))
            there = ((zm, up), (zp, lo), (xm, up), (xp, lo))
        else:
            here = ((zm, lo), (zp, up), (xm, lo), (xp, up))
            there = ((z2, lo), (z2, up), (x2, lo), (x2, up))
        to = to_x + to_z if kind < 2 else to_z + to_x
        copies = []
        for n, at in enumerate(here if sends else there):
            ref = (xa, xa, xc, xc)[n].at[(s,) + at]
            copies.append(rcopy(ref, ref, sx.at[s, kind, n], rx.at[s, kind, n], to[n]))
        return copies

    def start(s, *kinds):
        for kind in kinds:
            for c in gather(s, kind, True):
                c.start()

    def arrived(s, *kinds):
        for kind in kinds:
            for c in gather(s, kind, False):
                c.wait_recv()

    def exchange(s, m):
        return rcopy(
            part.at[s, 1 - k, m], pin.at[s, m], sp.at[s, m], rp.at[s, m], (partner, col)
        )

    def relay_copy(m, slot, to):
        return rcopy(part.at[0, k, m], relay.at[slot], sy.at[m], ry.at[slot], to)

    def relay_out(m):
        return relay_copy(m, k, (2 * yp, col) if m == 0 else (2 * ym + 1, col))

    def relay_in(slot):
        return relay_copy(0, slot, (partner, col))

    def reduce_out(s, m):
        q = yp + k * (ym - yp)
        return rcopy(
            part.at[s, k, m], rin.at[k, m], sr.at[s - 1, m], rr.at[k, m], (2 * q + s - 1, col)
        )

    def reduce_in(n, m):
        return rcopy(part.at[1, k, m], rin.at[n, m], sr.at[0, m], rr.at[n, m], (partner, col))

    def dots(s, m, first):
        rows_at = slice(m * HALF, (m + 1) * HALF)
        cut = slice(0, 6 * TILE) if first else slice(6 * TILE, 8 * TILE)
        hi = whi[rows_at, cut]
        both = jnp.concatenate([hi, wlo[rows_at, cut]], axis=0)
        both = jnp.dot(both, xhi[cut], preferred_element_type=F32)
        acc = jnp.dot(hi, xlo[cut], preferred_element_type=F32)
        acc += both[HALF:] + both[:HALF]
        for n in range(2):
            v = acc[:, n * LANES : (n + 1) * LANES]
            part[s, n, m] = v if first else part[s, n, m] + v

    def convert(v0, v1, at):
        v = jnp.concatenate([v0.reshape(TILE, LANES), v1.reshape(TILE, LANES)], axis=1)
        hi = v.astype(BF16)
        xhi[at, :] = hi
        xlo[at, :] = (v - hi.astype(F32)).astype(BF16)

    def convert_lines(s, low, high):
        @pl.loop(low, high)
        def _(n):
            zn, xn = (z + shift_of(n)) % 4, (x + shift_of(n)) % 4
            convert(xa[s, zn, :, 0], xa[s, zn, :, 1], place_a(n))
            convert(xc[s, xn, :, 0], xc[s, xn, :, 1], place_c(n))

    def near_part(s):
        convert_lines(s, 0, 3)
        dots(s, 0, True)
        dots(s, 1, True)

    def far_part(s):
        convert_lines(s, 3, 4)
        for m in range(2):
            dots(s, m, False)
            exchange(s, m).start()

    def row_sums(s):
        for m in range(2):
            exchange(s, m).wait_recv()
            part[s, k, m] = part[s, k, m] + pin[s, m]
            if s == 0:
                relay_out(m).start()
        if s > 0:
            relay_in(s - 1).wait_recv()
            part[s, k, k] = part[s, k, k] + relay[s - 1]
            for m in range(2):
                reduce_out(s, m).start()

    def back(m, j, slot):
        return rcopy(
            img.at[m, j], held[m].at[pl.ds(slot * 4, 4)], s4.at[m, j], r4.at[m, slot], (row, j)
        )

    def home(m, j, slot):
        return rcopy(
            ob.at[m, pl.ds(j * SLOTS, SLOTS)], fin.at[m, slot], s5.at[m, j], r5.at[m, slot],
            (row, j),
        )

    def finish(m):
        exchange(last, m).wait_recv()
        reduce_in(0, m).wait_recv()
        reduce_in(1, m).wait_recv()
        v = part[last, k, m] + pin[last, m] + rin[0, m] + rin[1, m]
        v = v.reshape(4, COLS, 1, 8, LANES)
        for b in range(4):
            img[m, :, b : b + 1] = v[b]

        @pl.loop(1, COLS)
        def _(d):
            back(m, (col + d) % COLS, col).start()

        held[m][pl.ds(col * 4, 4)] = img[m, col]

    def send_home(m):
        @pl.loop(1, COLS)
        def _(d):
            j = (col + COLS - d) % COLS
            back(m, j, j).wait_recv()

        @pl.loop(0, COLS * SLOTS, unroll=8)
        def _(i):
            ob[m, i] = held[m][jnp.maximum(tblk[i], 0)]

        @pl.loop(1, COLS)
        def _(d):
            home(m, (col + d) % COLS, col).start()

        fin[m, col] = ob[m, pl.ds(col * SLOTS, SLOTS)]

    rows_arrived(3)
    start(3, 0)
    rows_arrived(0)
    start(0, 0)
    rows_arrived(1)
    start(1, 0)
    arrived(3, 0)
    start(3, 1)
    rows_arrived(2)
    start(2, 0)
    for s in range(3):
        arrived(s, 0)
        start(s, 1)
    arrived(0, 1)
    start(0, 2, 3)
    arrived(1, 1)
    start(1, 2, 3)
    arrived(0, 2)
    start(0, 4)
    arrived(2, 1)
    start(2, 2, 3)
    arrived(0, 3)
    near_part(0)
    arrived(1, 2)
    start(1, 4)
    arrived(1, 3)
    near_part(1)
    arrived(0, 4)
    far_part(0)
    row_sums(0)
    arrived(2, 2)
    start(2, 4)
    arrived(3, 1)
    start(3, 2, 3)
    arrived(2, 3)
    near_part(2)
    arrived(1, 4)
    far_part(1)
    row_sums(1)
    arrived(2, 4)
    far_part(2)
    row_sums(2)
    arrived(3, 2)
    start(3, 4)
    arrived(3, 3)
    near_part(3)
    arrived(3, 4)
    far_part(3)
    finish(0)
    finish(1)
    send_home(0)
    send_home(1)

    @pl.loop(0, SLOTS)
    def _(s):
        diag = jnp.sum(
            jnp.where(row_iota == col_iota, energy[pl.ds(s, 1), :], 0.0), axis=1, keepdims=True
        )
        out[s] = diag * amp[s]

    for m in range(2):
        @pl.loop(1, COLS)
        def _(d):
            j = (col + COLS - d) % COLS
            home(m, j, j).wait_recv()

    @pl.loop(0, SLOTS)
    def _(s):
        live = (s < counts[col]).astype(F32)
        v = fin[:, :, pl.ds(s, 1)].reshape(TILE, LANES)
        returned = sum3(jnp.dot(onehot[s], split3(v), preferred_element_type=F32))
        out[s] = (returned + out[s]) * live

    @pl.loop(1, COLS)
    def _(d):
        j = (col + d) % COLS
        spread(j, col).wait_send()
        for m in range(2):
            back(m, j, col).wait_send()
            home(m, j, col).wait_send()

    for c in rows_sent:
        c.wait_send()

    for s in range(STEPS):
        for kind in range(5):
            for c in gather(s, kind, True):
                c.wait_send()
        for m in range(2):
            exchange(s, m).wait_send()
    for m in range(2):
        relay_out(m).wait_send()
        for s in (1, 2):
            reduce_out(s, m).wait_send()


def local(
    amplitudes, interaction, tile_counts, tile_block, recouple_sign, orbit_perm, particle_energy
):
    tiles = jnp.arange(64, dtype=jnp.int32)
    slots = jnp.arange(COLS * SLOTS, dtype=jnp.int32)
    hit = tile_block[None, :] == tiles[:, None]
    tile_of = jnp.sum(jnp.where(hit, slots[None, :], 0), axis=1)
    w = interaction.reshape(8, COLS, PIECE, 1024)
    smem = pl.BlockSpec(memory_space=pltpu.SMEM)
    vmem = pl.BlockSpec(memory_space=pltpu.VMEM)
    dma = pltpu.SemaphoreType.DMA
    return pl.pallas_call(
        kernel,
        out_shape=jax.ShapeDtypeStruct(amplitudes.shape, F32),
        in_specs=[smem] * 4 + [vmem] * 3 + [pl.BlockSpec(memory_space=pl.ANY)],
        out_specs=vmem,
        scratch_shapes=[
            pltpu.VMEM((SLOTS, TILE, TILE), BF16),
            pltpu.VMEM((COLS, SLOTS, PIECE, LANES), F32),
            pltpu.VMEM((COLS * SLOTS, PIECE, LANES), F32),
            pltpu.VMEM((64, PIECE, LANES), F32),
            pltpu.VMEM((STEPS, 4, 4, 2, 4, PIECE, LANES), F32),
            pltpu.VMEM((STEPS, 4, 4, 2, 4, PIECE, LANES), F32),
            pltpu.VMEM((4, 4, 8, PIECE, 1024), F32),
            pltpu.VMEM((1024, 2048), BF16),
            pltpu.VMEM((1024, 2048), BF16),
            pltpu.VMEM((2048, TILE), BF16),
            pltpu.VMEM((2048, TILE), BF16),
            pltpu.VMEM((STEPS, 2, 2, HALF, LANES), F32),
            pltpu.VMEM((STEPS, 2, HALF, LANES), F32),
            pltpu.VMEM((2, HALF, LANES), F32),
            pltpu.VMEM((2, 2, HALF, LANES), F32),
            pltpu.VMEM((2, COLS, 4, 8, LANES), F32),
            pltpu.VMEM((64, 8, LANES), F32),
            pltpu.VMEM((64, 8, LANES), F32),
            pltpu.VMEM((2, COLS * SLOTS, 8, LANES), F32),
            pltpu.VMEM((2, COLS, SLOTS, 8, LANES), F32),
            dma((COLS,)),
            dma((COLS,)), dma((COLS,)),
            dma((ROWS, 2)), dma((ROWS, 2)),
            dma((STEPS, 5, 4)), dma((STEPS, 5, 4)),
            dma((STEPS, 2)), dma((STEPS, 2)),
            dma((2,)), dma((2,)),
            dma((2, 2)), dma((2, 2)),
            dma((2, COLS)), dma((2, COLS)),
            dma((2, COLS)), dma((2, COLS)),
        ],
        compiler_params=pltpu.CompilerParams(
            collective_id=0, has_side_effects=True, vmem_limit_bytes=60 * 1024 * 1024
        ),
        name="sigma_step",
    )(tile_counts, tile_block, recouple_sign, tile_of, amplitudes, orbit_perm, particle_energy, w)


def solution(mesh):
    placed = (P("col", None, "row"), P("row", "col"), P(), P(), P(), P(), P("col", None))
    return jax.shard_map(
        local, mesh=mesh, in_specs=placed, out_specs=P("col", None, "row"), check_vma=False
    )
```

time: 109 us -> 102 us (0.936)
  Pallas kernels: 105 us -> 98.6 us
    pallas_call x1, Pallas kernels: 105 us -> 98.6 us  [local(): pl.pallas_call(kernel, out_shape=jax.ShapeDtypeStruct(amplitudes.shape, F...]
where the time goes in v3:
time: 102 us
  Pallas kernels  98.6 us (97%)
  local copies, waits for them, and re-layouts  2.06 us (2%)
  other arithmetic  1.28 us (1%)
    pallas_call x1, Pallas kernels, local(): pl.pallas_call(kernel, out_shape=jax.ShapeDtypeStruct(amplitudes.shape, F...  98.6 us
    unnamed x1, local copies, waits for them, and re-layouts  2.06 us

profile of v3, /device:TPU:0, one launch (start us, length us, event | category | flops | bytes accessed | tf_op | source)
XLA Modules:
  0.0 102.0 jit_solution(11907999761357780995)
XLA Ops:
  0.0 1.3 %select_reduce_fusion.tile_of = s32[64]{0:T(128)} fusion(s32[96]{0:T(128)} %tblk.1), kind=kLoop, calls=%fused_computation | loop fusion | flops 18368 | bytes 640 | tf_op jit(solution)/shard_map/reduce_sum | solution.py:425
  1.3 98.6 %sigma_step.1 = f32[6,256,128]{2,1,0:T(8,128)} custom-call(s32[16]{0:T(128)} %counts.1, s32[96]{0:T(128)} %tblk.1, s32[96]{0:T(128)} %signs.1, s32[64]{0:T(128)} %select_reduce_fusion.tile_of, f32[6,256,128]{2,1,0:T(8,128)} %amp.1, s32[96,256]{1,0:T(8,128)} %perm.1, f32[6,256]{1,0:T(8,128)} %energy.1, f32[8,16,16,1024]{3,2,1,0:T(8,128)} %bitcast.1), custom_call_target="tpu_custom_call" | custom-call | tf_op jit(solution)/shard_map/sigma_step/pallas_call | solution.py:430
  99.9 2.1 %copy.9 = f32[6,256,128]{2,1,0:T(8,128)} copy(f32[6,256,128]{2,1,0:T(8,128)} %sigma_step.1) | data formatting | bytes 1572864

commit v4 on v3

--- a/solution.py
+++ b/solution.py
@@ -29,10 +29,10 @@
 
 
 def kernel(
-    counts, tblk, signs, tile_of, amp, perm, energy, w_hbm, out,
+    counts, tblk, signs, amp, perm, energy, w_hbm, out, slot_row, slot_of,
     onehot, send1, recv1, sel, xa, xc, wst, whi, wlo, xhi, xlo, part, pin, relay, rin,
     img, gb0, gb1, ob, fin,
-    wsem, s1, r1, s2, r2, sx, rx, sp, rp, sy, ry, sr, rr, s4, r4, s5, r5,
+    isem, wsem, s1, r1, s2, r2, sx, rx, sp, rp, sy, ry, sr, rr, s4, r4, s5, r5,
 ):
     row, col = lax.axis_index("row"), lax.axis_index("col")
     y, k = row // 2, row % 2
@@ -67,6 +67,14 @@
     def _(j):
         wcopy(j).start()
 
+    lane = lax.broadcasted_iota(jnp.int32, (8, LANES), 1)
+    found = jnp.zeros((8, LANES), jnp.int32)
+    for i in range(COLS * SLOTS):
+        found = jnp.where(lane == tblk[i], i, found)
+    slot_row[...] = found
+    to_scalars = pltpu.make_async_copy(slot_row, slot_of, isem)
+    to_scalars.start()
+
     row_iota = lax.broadcasted_iota(jnp.int32, (TILE, TILE), 0)
     col_iota = lax.broadcasted_iota(jnp.int32, (TILE, TILE), 1)
 
@@ -129,9 +137,11 @@
         j = (col + COLS - d) % COLS
         spread(j, j).wait_recv()
 
-    @pl.loop(0, 64, unroll=8)
+    to_scalars.wait()
+
+    @pl.loop(0, 64, unroll=32)
     def _(g):
-        sel[g] = recv1[tile_of[g]]
+        sel[g] = recv1[slot_of[0, g]]
 
     def rows_copies(r, source, slot):
         return [
@@ -273,10 +283,12 @@
             if s == 0:
                 relay_out(m).start()
         if s > 0:
-            relay_in(s - 1).wait_recv()
-            part[s, k, k] = part[s, k, k] + relay[s - 1]
-            for m in range(2):
-                reduce_out(s, m).start()
+            reduce_out(s, 1 - k).start()
+
+    def relay_sum(s):
+        relay_in(s - 1).wait_recv()
+        part[s, k, k] = part[s, k, k] + relay[s - 1]
+        reduce_out(s, k).start()
 
     def back(m, j, slot):
         return rcopy(
@@ -310,7 +322,7 @@
             j = (col + COLS - d) % COLS
             back(m, j, j).wait_recv()
 
-        @pl.loop(0, COLS * SLOTS, unroll=8)
+        @pl.loop(0, COLS * SLOTS, unroll=32)
         def _(i):
             ob[m, i] = held[m][jnp.maximum(tblk[i], 0)]
 
@@ -336,32 +348,36 @@
     arrived(0, 1)
     start(0, 2, 3)
     arrived(1, 1)
-    start(1, 2, 3)
+    start(1, 2)
     arrived(0, 2)
     start(0, 4)
+    start(1, 3)
     arrived(2, 1)
-    start(2, 2, 3)
+    start(2, 2)
     arrived(0, 3)
     near_part(0)
     arrived(1, 2)
     start(1, 4)
-    arrived(1, 3)
-    near_part(1)
+    start(2, 3)
     arrived(0, 4)
     far_part(0)
     row_sums(0)
+    arrived(1, 3)
+    near_part(1)
     arrived(2, 2)
     start(2, 4)
     arrived(3, 1)
     start(3, 2, 3)
-    arrived(2, 3)
-    near_part(2)
     arrived(1, 4)
     far_part(1)
     row_sums(1)
+    arrived(2, 3)
+    relay_sum(1)
+    near_part(2)
     arrived(2, 4)
     far_part(2)
     row_sums(2)
+    relay_sum(2)
     arrived(3, 2)
     start(3, 4)
     arrived(3, 3)
@@ -373,25 +389,27 @@
     send_home(0)
     send_home(1)
 
-    @pl.loop(0, SLOTS)
-    def _(s):
-        diag = jnp.sum(
-            jnp.where(row_iota == col_iota, energy[pl.ds(s, 1), :], 0.0), axis=1, keepdims=True
-        )
-        out[s] = diag * amp[s]
-
-    for m in range(2):
+    def homed(m):
         @pl.loop(1, COLS)
         def _(d):
             j = (col + COLS - d) % COLS
             home(m, j, j).wait_recv()
 
-    @pl.loop(0, SLOTS)
-    def _(s):
+    def returned(s, m):
+        v = fin[m, :, s].reshape(LANES, LANES)
+        hot = onehot[s, :, m * LANES : (m + 1) * LANES]
+        return sum3(jnp.dot(hot, split3(v), preferred_element_type=F32))
+
+    homed(0)
+    for s in range(SLOTS):
+        diag = jnp.sum(
+            jnp.where(row_iota == col_iota, energy[s : s + 1, :], 0.0), axis=1, keepdims=True
+        )
+        out[s] = diag * amp[s] + returned(s, 0)
+    homed(1)
+    for s in range(SLOTS):
         live = (s < counts[col]).astype(F32)
-        v = fin[:, :, pl.ds(s, 1)].reshape(TILE, LANES)
-        returned = sum3(jnp.dot(onehot[s], split3(v), preferred_element_type=F32))
-        out[s] = (returned + out[s]) * live
+        out[s] = (out[s] + returned(s, 1)) * live
 
     @pl.loop(1, COLS)
     def _(d):
@@ -419,10 +437,6 @@
 def local(
     amplitudes, interaction, tile_counts, tile_block, recouple_sign, orbit_perm, particle_energy
 ):
-    tiles = jnp.arange(64, dtype=jnp.int32)
-    slots = jnp.arange(COLS * SLOTS, dtype=jnp.int32)
-    hit = tile_block[None, :] == tiles[:, None]
-    tile_of = jnp.sum(jnp.where(hit, slots[None, :], 0), axis=1)
     w = interaction.reshape(8, COLS, PIECE, 1024)
     smem = pl.BlockSpec(memory_space=pltpu.SMEM)
     vmem = pl.BlockSpec(memory_space=pltpu.VMEM)
@@ -430,9 +444,11 @@
     return pl.pallas_call(
         kernel,
         out_shape=jax.ShapeDtypeStruct(amplitudes.shape, F32),
-        in_specs=[smem] * 4 + [vmem] * 3 + [pl.BlockSpec(memory_space=pl.ANY)],
+        in_specs=[smem] * 3 + [vmem] * 3 + [pl.BlockSpec(memory_space=pl.ANY)],
         out_specs=vmem,
         scratch_shapes=[
+            pltpu.VMEM((8, LANES), jnp.int32),
+            pltpu.SMEM((8, LANES), jnp.int32),
             pltpu.VMEM((SLOTS, TILE, TILE), BF16),
             pltpu.VMEM((COLS, SLOTS, PIECE, LANES), F32),
             pltpu.VMEM((COLS * SLOTS, PIECE, LANES), F32),
@@ -453,6 +469,7 @@
             pltpu.VMEM((64, 8, LANES), F32),
             pltpu.VMEM((2, COLS * SLOTS, 8, LANES), F32),
             pltpu.VMEM((2, COLS, SLOTS, 8, LANES), F32),
+            dma,
             dma((COLS,)),
             dma((COLS,)), dma((COLS,)),
             dma((ROWS, 2)), dma((ROWS, 2)),
@@ -467,7 +484,7 @@
             collective_id=0, has_side_effects=True, vmem_limit_bytes=60 * 1024 * 1024
         ),
         name="sigma_step",
-    )(tile_counts, tile_block, recouple_sign, tile_of, amplitudes, orbit_perm, particle_energy, w)
+    )(tile_counts, tile_block, recouple_sign, amplitudes, orbit_perm, particle_energy, w)
 
 
 def solution(mesh):

time: 102 us -> 101 us (level)
  other arithmetic: 1.28 us -> 0 us
    reduce_sum x1 -> x0, other arithmetic: 1.28 us -> none  [local(): tile_of = jnp.sum(jnp.where(hit, slots[None, :], 0), axis=1)]
where the time goes in v4:
time: 101 us; the launch traced here: 100 us
  Pallas kernels  98.1 us (97%)
  local copies, waits for them, and re-layouts  2.06 us (2%)
    pallas_call x1, Pallas kernels, local(): pl.pallas_call(kernel, out_shape=jax.ShapeDtypeStruct(amplitudes.shape, F...  98.1 us
    unnamed x1, local copies, waits for them, and re-layouts  2.06 us

profile of v4, /device:TPU:0, one launch (start us, length us, event | category | flops | bytes accessed | tf_op | source)
XLA Modules:
  0.0 100.2 jit_solution(2892801153971030240)
XLA Ops:
  0.0 98.1 %sigma_step.1 = f32[6,256,128]{2,1,0:T(8,128)} custom-call(s32[16]{0:T(128)} %counts.1, s32[96]{0:T(128)} %tblk.1, s32[96]{0:T(128)} %signs.1, f32[6,256,128]{2,1,0:T(8,128)} %amp.1, s32[96,256]{1,0:T(8,128)} %perm.1, f32[6,256]{1,0:T(8,128)} %energy.1, f32[8,16,16,1024]{3,2,1,0:T(8,128)} %bitcast.1), custom_call_target="tpu_custom_call" | custom-call | tf_op jit(solution)/shard_map/sigma_step/pallas_call | solution.py:444
  98.1 2.1 %copy.9 = f32[6,256,128]{2,1,0:T(8,128)} copy(f32[6,256,128]{2,1,0:T(8,128)} %sigma_step.1) | data formatting | bytes 1572864

commit v5 on v4

--- a/solution.py
+++ b/solution.py
@@ -139,9 +139,13 @@
 
     to_scalars.wait()
 
-    @pl.loop(0, 64, unroll=32)
-    def _(g):
-        sel[g] = recv1[slot_of[0, g]]
+    def select(first, count):
+        @pl.loop(0, count, unroll=16)
+        def _(n):
+            g = (first + n) % 64
+            sel[g] = recv1[slot_of[0, g]]
+
+    select(16 * y2, 16)
 
     def rows_copies(r, source, slot):
         return [
@@ -165,7 +169,10 @@
         )
         for c in rows_copies(r, row, slot)
     ]
-    for c in rows_sent:
+    for c in rows_sent[:4]:
+        c.start()
+    select(16 * y2 + 16, 48)
+    for c in rows_sent[4:]:
         c.start()
 
     xa[3, z, x, k] = sel[pl.ds(row * 8, 4)]

time: 101 us -> 101 us (level)
  no operation moved by 1% of the time
where the time goes in v5:
time: 101 us; the launch traced here: 100 us
  Pallas kernels  98.1 us (97%)
  local copies, waits for them, and re-layouts  2.06 us (2%)
    pallas_call x1, Pallas kernels, local(): pl.pallas_call(kernel, out_shape=jax.ShapeDtypeStruct(amplitudes.shape, F...  98.1 us
    unnamed x1, local copies, waits for them, and re-layouts  2.06 us

profile of v5, /device:TPU:0, one launch (start us, length us, event | category | flops | bytes accessed | tf_op | source)
XLA Modules:
  0.0 100.2 jit_solution(16155224445781731852)
XLA Ops:
  0.0 98.1 %sigma_step.1 = f32[6,256,128]{2,1,0:T(8,128)} custom-call(s32[16]{0:T(128)} %counts.1, s32[96]{0:T(128)} %tblk.1, s32[96]{0:T(128)} %signs.1, f32[6,256,128]{2,1,0:T(8,128)} %amp.1, s32[96,256]{1,0:T(8,128)} %perm.1, f32[6,256]{1,0:T(8,128)} %energy.1, f32[8,16,16,1024]{3,2,1,0:T(8,128)} %bitcast.1), custom_call_target="tpu_custom_call" | custom-call | tf_op jit(solution)/shard_map/sigma_step/pallas_call | solution.py:451
  98.1 2.1 %copy.9 = f32[6,256,128]{2,1,0:T(8,128)} copy(f32[6,256,128]{2,1,0:T(8,128)} %sigma_step.1) | data formatting | bytes 1572864
